TPU v7x, 32 devices: a whole 2x2x4 slice. The times are simulated.
32 devices in a mesh: prow: 8 (over z, x), pcol: 4 (over y, core).
Axes of the slice: x: 2, y: 2, z: 4, core: 2. Of those that a mesh axis runs over, the one named last changes fastest.
Arguments:
- sigma_top: bfloat16 [8, 8, 128, 128], P('prow', 'pcol'), may hold values from -6 to 6
- factor_one: bfloat16 [8, 8, 128, 128], P('prow', 'pcol'), may hold values from -0.1875 to 0.1875
- inverse_one: bfloat16 [8, 128, 128], P('prow'), may hold values from -0.5 to 0.5
- pattern_one: int32 [8, 8], replicated, may hold values from 0 to 7, as said below
- factor_two: bfloat16 [8, 8, 128, 128], P('prow', 'pcol'), may hold values from -0.25 to 0.25
- parent_block: bfloat16 [8, 128, 128], P('prow'), may hold values from -0.25 to 0.25
- inverse_two: bfloat16 [8, 128, 128], P('prow'), may hold values from -0.5 to 0.5
- parent_two: int32 [8], replicated, may hold values from 0 to 7
- keep_two: int32 [8, 8], replicated, may hold values 0 or 1
Outputs:
- inverse_top_one: bfloat16 [8, 8, 128, 128], P('prow')
- diag_one: float32 [8, 128, 128], P('prow')
- inverse_top_two: bfloat16 [8, 8, 128, 128], P('prow')
- inverse_parent_two: float32 [8, 128, 128], P('prow')
- diag_two: float32 [8, 128, 128], P('prow')
Inputs may be any that keep to these rules, and one draw needn't show every extreme that they name: Each row of pattern_one lists 8 distinct block rows of the top region. keep_two[i, k] = 1 where level-two supernode i's pattern holds the k-th tile of its parent's pattern. parent_two names level-one supernodes.
All inputs are finite; a program needn't handle non-finite values.
Results may differ from a plain program's by a relative error of at most 0.023.
Values may be sent and summed in bfloat16 or wider, within the bound.
A program may use at most 64 MiB of HBM per device.

v0:
```python
import jax
import jax.numpy as jnp
from jax import lax
from jax.sharding import PartitionSpec as P

highest = lax.Precision.HIGHEST


def split_product(form, left, right):
    upper_part = right.astype(jnp.bfloat16)
    lower_part = (right - upper_part.astype(jnp.float32)).astype(jnp.bfloat16)
    first = jnp.einsum(form, left, upper_part, preferred_element_type=jnp.float32)
    return first + jnp.einsum(form, left, lower_part, preferred_element_type=jnp.float32)


def body(
    sigma_top,
    factor_one,
    inverse_one,
    pattern_one,
    factor_two,
    parent_block,
    inverse_two,
    parent_two,
    keep_two,
):
    rows_here = sigma_top.shape[0]
    cols_here = sigma_top.shape[1]
    tile_width = sigma_top.shape[2]
    prow_index = lax.axis_index("prow")
    pcol_index = lax.axis_index("pcol")
    first_row = prow_index * rows_here
    column_ids = pcol_index * cols_here + jnp.arange(cols_here, dtype=jnp.int32)
    top_rows = first_row + jnp.arange(rows_here, dtype=jnp.int32)
    owner_column = first_row // cols_here
    diagonal_owner = owner_column == pcol_index
    offset = jnp.clip(first_row - pcol_index * cols_here, 0, cols_here - rows_here)
    total_one = pattern_one.shape[0]
    local_one = factor_one.shape[0]
    lower_one = jnp.tril(inverse_one)
    scaled_local = jnp.einsum(
        "jkwv,jvx->jkwx", factor_one, lower_one, preferred_element_type=jnp.float32
    ).astype(jnp.bfloat16)
    scaled_rows = lax.all_gather(scaled_local, "pcol", axis=1, tiled=True)
    own_pattern = lax.dynamic_slice_in_dim(pattern_one, prow_index * local_one, local_one, 0)
    picker_one = (own_pattern[:, :, None] == column_ids[None, None, :]).astype(jnp.bfloat16)
    spread_one = jnp.einsum(
        "jkc,jkwv->jcwv", picker_one, scaled_rows, preferred_element_type=jnp.float32
    ).astype(jnp.bfloat16)
    spread_all = lax.all_gather(spread_one, "prow", axis=0, tiled=True)
    partial_one = jnp.einsum(
        "acwv,jcvx->ajwx", sigma_top, spread_all, preferred_element_type=jnp.float32
    )
    summed_one = lax.psum(partial_one.astype(jnp.bfloat16), "pcol").astype(jnp.float32)
    member_one = jnp.sum(
        (pattern_one[None, :, :] == top_rows[:, None, None]).astype(jnp.float32), axis=2
    )
    inverse_top_one = (-summed_one * member_one[:, :, None, None]).astype(jnp.bfloat16)
    own_rows = lax.dynamic_slice_in_dim(spread_all, offset, rows_here, 1)
    quadratic_one = split_product("jawv,ajwx->jvx", own_rows, summed_one)
    quadratic_one = jnp.where(diagonal_owner, quadratic_one, 0.0)
    lower_float = lower_one.astype(jnp.float32)
    gram_one = jnp.einsum("jwv,jwx->jvx", lower_float, lower_float, precision=highest)
    placed = lax.dynamic_update_slice_in_dim(
        jnp.zeros((total_one, tile_width, tile_width), jnp.float32),
        gram_one,
        prow_index * local_one,
        0,
    )
    partial_diag = quadratic_one + jnp.where(pcol_index == 0, placed, 0.0)
    diagonal_all = lax.psum(partial_diag, ("prow", "pcol"))
    diag_one = lax.dynamic_slice_in_dim(diagonal_all, prow_index * local_one, local_one, 0)
    local_two = factor_two.shape[0]
    lower_two = jnp.tril(inverse_two)
    scaled_two = jnp.einsum(
        "ikwv,ivx->ikwx", factor_two, lower_two, preferred_element_type=jnp.float32
    ).astype(jnp.bfloat16)
    scaled_parent = jnp.einsum(
        "iwv,ivx->iwx", parent_block, lower_two, preferred_element_type=jnp.float32
    ).astype(jnp.bfloat16)
    scaled_rows_two = lax.all_gather(scaled_two, "pcol", axis=1, tiled=True)
    parent_hot = (parent_two[:, None] == jnp.arange(total_one, dtype=jnp.int32)[None, :]).astype(
        jnp.int32
    )
    parent_pattern = jnp.sum(parent_hot[:, :, None] * pattern_one[None, :, :], axis=1)
    own_parent_pattern = lax.dynamic_slice_in_dim(
        parent_pattern, prow_index * local_two, local_two, 0
    )
    own_keep = lax.dynamic_slice_in_dim(keep_two, prow_index * local_two, local_two, 0)
    picker_two = (
        (own_parent_pattern[:, :, None] == column_ids[None, None, :]).astype(jnp.int32)
        * own_keep[:, :, None]
    ).astype(jnp.bfloat16)
    spread_two = jnp.einsum(
        "ikc,ikwv->icwv", picker_two, scaled_rows_two, preferred_element_type=jnp.float32
    ).astype(jnp.bfloat16)
    spread_all_two, parent_all = (
        lax.all_gather(spread_two, "prow", axis=0, tiled=True),
        lax.all_gather(scaled_parent, "prow", axis=0, tiled=True),
    )
    partial_two = jnp.einsum(
        "acwv,icvx->aiwx", sigma_top, spread_all_two, preferred_element_type=jnp.float32
    )
    inherited = jnp.einsum(
        "ij,ajwv->aiwv",
        parent_hot.astype(jnp.bfloat16),
        inverse_top_one,
        preferred_element_type=jnp.float32,
    ).astype(jnp.bfloat16)
    carried_rows = jnp.einsum(
        "aiwv,ivx->aiwx", inherited, parent_all, preferred_element_type=jnp.float32
    )
    partial_two = partial_two + jnp.where(diagonal_owner, carried_rows, 0.0)
    summed_two = lax.psum(partial_two.astype(jnp.bfloat16), "pcol").astype(jnp.float32)
    member_two = jnp.sum(
        (parent_pattern[None, :, :] == top_rows[:, None, None]).astype(jnp.float32)
        * keep_two[None, :, :].astype(jnp.float32),
        axis=2,
    )
    inverse_top_two = (-summed_two * member_two[:, :, None, None]).astype(jnp.bfloat16)
    own_two = lax.dynamic_slice_in_dim(spread_all_two, offset, rows_here, 1)
    cross = jnp.einsum("aiwv,iawx->ivx", inherited, own_two, preferred_element_type=jnp.float32)
    quadratic_two = split_product("iawv,aiwx->ivx", own_two, summed_two)
    cross = jnp.where(diagonal_owner, cross, 0.0)
    quadratic_two = jnp.where(diagonal_owner, quadratic_two, 0.0)
    cross_part, quadratic_part = (
        lax.psum_scatter(
            cross.astype(jnp.bfloat16), "prow", scatter_dimension=0, tiled=True
        ).astype(jnp.float32),
        lax.psum_scatter(
            quadratic_two.astype(jnp.bfloat16), "prow", scatter_dimension=0, tiled=True
        ).astype(jnp.float32),
    )
    cross_sum, quadratic_sum = (
        lax.psum(cross_part.astype(jnp.bfloat16), "pcol").astype(jnp.float32),
        lax.psum(quadratic_part.astype(jnp.bfloat16), "pcol").astype(jnp.float32),
    )
    own_hot = lax.dynamic_slice_in_dim(parent_hot, prow_index * local_two, local_two, 0).astype(
        jnp.float32
    )
    parent_diag = jnp.einsum("ij,jwv->iwv", own_hot, diagonal_all, precision=highest)
    parent_float = scaled_parent.astype(jnp.float32)
    carried = cross_sum + jnp.einsum("iwv,ivx->iwx", parent_diag, parent_float, precision=highest)
    lower_two_float = lower_two.astype(jnp.float32)
    diag_two = jnp.einsum("iwv,iwx->ivx", lower_two_float, lower_two_float, precision=highest)
    diag_two = (
        diag_two
        + quadratic_sum
        + jnp.einsum("iwv,iwx->ivx", parent_float, carried, precision=highest)
    )
    return (inverse_top_one, diag_one, inverse_top_two, -carried, diag_two)


def solution(mesh):
    in_specs = (
        P("prow", "pcol", None, None),
        P("prow", "pcol", None, None),
        P("prow", None, None),
        P(),
        P("prow", "pcol", None, None),
        P("prow", None, None),
        P("prow", None, None),
        P(),
        P(),
    )
    out_specs = (
        P("prow", None, None, None),
        P("prow", None, None),
        P("prow", None, None, None),
        P("prow", None, None),
        P("prow", None, None),
    )
    return jax.shard_map(body, mesh=mesh, in_specs=in_specs, out_specs=out_specs, check_vma=False)
```

profile of v0, /device:TPU:0, one launch (start us, length us, event | category | flops | bytes accessed | tf_op | source)
XLA Modules:
  0.0 453.0 jit_solution(8151209483114322396)
XLA Ops:
  7.2 1.1 fusion.10
  8.4 7.2 %all-gather = bf16[8,128,128]{2,1,0:T(8,128)(2,1)S(1)} all-gather(bf16[2,128,128]{2,1,0:T(8,128)(2,1)S(1)} %copy.72), channel_id=2, replica_groups=mesh['prow'=8,'pcol'=4] {'pcol'}, dimensions={0}, use_global_device_ids=true | all-gather | bytes 327680 | tf_op jit(solution)/shard_map/all_gather | solution.py:44
  16.0 31.9 %all-gather.1 = bf16[16,128,128]{2,1,0:T(8,128)(2,1)S(1)} all-gather(bf16[2,128,128]{2,1,0:T(8,128)(2,1)S(1)} %copy.74), channel_id=3, replica_groups=mesh['prow'=8,'pcol'=4] {'prow'}, dimensions={0}, use_global_device_ids=true | all-gather | bytes 589824 | tf_op jit(solution)/shard_map/all_gather | solution.py:50
  47.9 1.1 fusion.7
  50.9 5.8 %all-gather.2 = bf16[8,128,128]{2,1,0:T(8,128)(2,1)S(1)} all-gather(bf16[2,128,128]{2,1,0:T(8,128)(2,1)S(1)} %copy.79), channel_id=4, replica_groups=mesh['prow'=8,'pcol'=4] {'pcol'}, dimensions={0}, use_global_device_ids=true | all-gather | bytes 327680 | tf_op jit(solution)/shard_map/all_gather | solution.py:81
  57.0 31.5 %all-gather.3 = bf16[16,128,128]{2,1,0:T(8,128)(2,1)S(1)} all-gather(bf16[2,128,128]{2,1,0:T(8,128)(2,1)S(1)} %copy.81), channel_id=5, replica_groups=mesh['prow'=8,'pcol'=4] {'prow'}, dimensions={0}, use_global_device_ids=true | all-gather | bytes 589824 | tf_op jit(solution)/shard_map/all_gather | solution.py:98
  88.7 26.4 %all-gather.4 = bf16[1024,128]{0,1:T(8,128)(2,1)S(1)} all-gather(bf16[128,128]{0,1:T(8,128)(2,1)S(1)} %bitcast.162), channel_id=6, replica_groups=mesh['prow'=8,'pcol'=4] {'prow'}, dimensions={0}, use_global_device_ids=true | all-gather | bytes 294912 | tf_op jit(solution)/shard_map/all_gather | solution.py:99
  115.5 1.1 fusion.112
  117.2 0.9 fusion.9
  118.2 0.9 copy-done.1
  121.5 1.0 fusion.6
  122.7 26.8 %all-reduce.10.cloned.1.call-done = bf16[1,8,128,128]{2,3,1,0:T(8,128)(2,1)} async-done(((bf16[1,8,128,128]{2,3,1,0:T(8,128)(2,1)}), bf16[1,8,128,128]{2,3,1,0:T(8,128)(2,1)}) %all-reduce.10.cloned.1.call-update) | async-done | bytes 262160 | tf_op jit(solution)/shard_map/psum | solution.py:114
  149.5 1.3 fusion.32
  150.9 1.0 fusion.3
  152.1 0.9 copy.92
  153.0 0.9 copy.93
  153.9 128.7 %all-reduce.8.cloned.1.call-done = f32[8,128,128]{2,1,0:T(8,128)} async-done(((f32[8,128,128]{2,1,0:T(8,128)}), f32[8,128,128]{2,1,0:T(8,128)}) %all-reduce.8.cloned.1.call-update) | async-done | bytes 524304 | tf_op jit(solution)/shard_map/psum | solution.py:71
  282.6 1.8 fusion.24
  284.5 61.9 %reduce-scatter.3.cloned.1.call-done = bf16[1,128,128]{2,1,0:T(8,128)(2,1)} async-done(((bf16[8,128,128]{2,1,0:T(8,128)(2,1)}), bf16[1,128,128]{2,1,0:T(8,128)(2,1)}) %reduce-scatter.3.cloned.1.call-update) | async-done | bytes 32784 | tf_op jit(solution)/shard_map/reduce_scatter | solution.py:127
  346.4 63.8 %reduce-scatter.5.cloned.1.call-done = bf16[1,128,128]{2,1,0:T(8,128)(2,1)} async-done(((bf16[8,128,128]{2,1,0:T(8,128)(2,1)}), bf16[1,128,128]{2,1,0:T(8,128)(2,1)}) %reduce-scatter.5.cloned.1.call-update) | async-done | bytes 32784 | tf_op jit(solution)/shard_map/reduce_scatter | solution.py:130
  410.3 1.5 constant_dynamic-slice_fusion.3
  411.8 31.2 %all-reduce.12.cloned.1.call-done = (bf16[1,128,128]{2,1,0:T(8,128)(2,1)}, bf16[1,128,128]{2,1,0:T(8,128)(2,1)}) async-done(((bf16[1,128,128]{2,1,0:T(8,128)(2,1)}, bf16[1,128,128]{2,1,0:T(8,128)(2,1)}), (bf16[1,128,128]{2,1,0:T(8,128)(2,1)}, bf16[1,128,128]{2,1,0:T(8,128)(2,1)})) %all-reduce.12.cloned.1.call-update) | async-done | bytes 65552 | tf_op jit(solution)/shard_map/psum | solution.py:135
  442.9 1.6 fusion.102
  445.3 0.8 fusion.15
  (64 shorter events, 7.6 us)
Async XLA Ops:
  7.2 40.7 %copy-start = (bf16[1,2,128,128]{3,2,1,0:T(8,128)(2,1)S(1)}, bf16[1,2,128,128]{3,2,1,0:T(8,128)(2,1)}, u32[]{:S(2)}) copy-start(bf16[1,2,128,128]{3,2,1,0:T(8,128)(2,1)} %param.9) | copy-start | bytes 196612
  7.2 108.3 %all-reduce.6.cloned.1.call-start = ((), (), s32[]{:S(2)}) async-start(), calls=%async_computation.2 | async-start | bytes 524288 | tf_op jit(solution)/shard_map/psum | solution.py:54
  8.4 7.2 %copy-start.9 = (s32[8,8]{1,0:T(8,128)S(1)}, s32[8,8]{1,0:T(8,128)}, u32[]{:S(2)}) copy-start(s32[8,8]{1,0:T(8,128)} %param.12) | copy-start | bytes 772
  48.9 100.6 %all-reduce.10.cloned.1.call-start = ((), (), s32[]{:S(2)}) async-start(), calls=%async_computation.4 | async-start | bytes 524288 | tf_op jit(solution)/shard_map/psum | solution.py:114
  49.1 0.7 copy-start.11
  49.1 1.4 copy-start.6
  49.4 1.1 copy-start.4
  49.8 0.7 copy-start.10
  57.0 31.5 %copy-start.7 = (bf16[1,128,128]{2,1,0:T(8,128)(2,1)S(1)}, bf16[1,128,128]{2,1,0:T(8,128)(2,1)}, u32[]{:S(2)}) copy-start(bf16[1,128,128]{2,1,0:T(8,128)(2,1)} %param.14) | copy-start | bytes 98308
  118.2 0.9 copy-start.1
  118.2 164.4 %all-reduce.8.cloned.1.call-start = ((), (), s32[]{:S(2)}) async-start(), calls=%async_computation.3 | async-start | bytes 1048576 | tf_op jit(solution)/shard_map/psum | solution.py:71
  119.4 0.8 copy-start.5
  120.4 0.8 copy-start.2
  121.2 225.2 %reduce-scatter.3.cloned.1.call-start = ((), (), s32[]{:S(2)}) async-start(), calls=%async_computation.5 | async-start | bytes 294912 | tf_op jit(solution)/shard_map/reduce_scatter | solution.py:127
  122.6 287.7 %reduce-scatter.5.cloned.1.call-start = ((), (), s32[]{:S(2)}) async-start(), calls=%async_computation.6 | async-start | bytes 294912 | tf_op jit(solution)/shard_map/reduce_scatter | solution.py:130
  149.5 1.3 copy-start.3
  151.9 291.0 %all-reduce.12.cloned.1.call-start = ((), (), s32[]{:S(2)}) async-start(), calls=%async_computation.7 | async-start | bytes 131072 | tf_op jit(solution)/shard_map/psum | solution.py:135
  444.5 0.8 copy-start.8
Sparse Core Ops, SparseCore 0:
  49.1 32.7 all-reduce.5
  118.3 31.1 all-reduce.9
  154.8 127.7 all-reduce.7
  286.2 60.2 reduce-scatter.2
  350.0 60.2 reduce-scatter.4
  412.6 30.2 all-reduce.11
where the time goes:
time: 454 us; the launch traced here: 453 us
  waiting for transfers between devices  313 us (69%)
  blocking collectives  103 us (23%)
  between operations  14.4 us (3%)
  matrix products  13.2 us (3%)
  local copies, waits for them, and re-layouts  8.08 us (2%)
    psum x1, waiting for transfers between devices, body(): diagonal_all = lax.psum(partial_diag, ('prow', 'pcol'))  129 us
    reduce_scatter x1, waiting for transfers between devices, body(): lax.psum_scatter(quadratic_two.astype(jnp.bfloat16), 'prow', scatter_dime...  63.8 us
    reduce_scatter x1, waiting for transfers between devices, body(): lax.psum_scatter(cross.astype(jnp.bfloat16), 'prow', scatter_dimension=0,...  61.9 us
    all_gather x1, blocking collectives, body(): spread_all = lax.all_gather(spread_one, 'prow', axis=0, tiled=True)  31.9 us
    all_gather x1, blocking collectives, body(): lax.all_gather(spread_two, 'prow', axis=0, tiled=True)  31.5 us
    psum x1, waiting for transfers between devices, body(): lax.psum(cross_part.astype(jnp.bfloat16), 'pcol').astype(jnp.float32)  31.2 us
    psum x1, waiting for transfers between devices, body(): lax.psum(partial_two.astype(jnp.bfloat16), 'pcol').astype(jnp.float32)  26.8 us
    all_gather x1, blocking collectives, body(): lax.all_gather(scaled_parent, 'prow', axis=0, tiled=True)  26.4 us
  transfers between devices with their start and end apart: 6, of which 5 were waited for; matrix products, arithmetic and copies ran while one was open for 3% of the time, Pallas kernels for 0%

commit v1 on v0

--- a/solution.py
+++ b/solution.py
@@ -132,7 +132,9 @@
         ).astype(jnp.float32),
     )
     cross_sum, quadratic_sum = (
-        lax.psum(cross_part.astype(jnp.bfloat16), "pcol").astype(jnp.float32),
+        jnp.sum(lax.all_gather(cross_part.astype(jnp.bfloat16), "pcol"), axis=0).astype(
+            jnp.float32
+        ),
         lax.psum(quadratic_part.astype(jnp.bfloat16), "pcol").astype(jnp.float32),
     )
     own_hot = lax.dynamic_slice_in_dim(parent_hot, prow_index * local_two, local_two, 0).astype(

time: 454 us -> 429 us (0.945)
  waiting for transfers between devices: 313 us -> 274 us
  blocking collectives: 103 us -> 119 us
    psum x1 -> x0, waiting for transfers between devices: 31.2 us -> none  [body(): lax.psum(cross_part.astype(jnp.bfloat16), 'pcol').astype(jnp.float32)]
    psum x0 -> x1, blocking collectives: none -> 10.8 us  [body(): lax.psum(quadratic_part.astype(jnp.bfloat16), 'pcol').astype(jnp.float32)]
    reduce_scatter x1, waiting for transfers between devices: 63.8 us -> 57.2 us  [body(): lax.psum_scatter(quadratic_two.astype(jnp.bfloat16), 'prow', scatter_dime...]
    all_gather x0 -> x1, blocking collectives: none -> 5.62 us  [body(): lax.all_gather(cross_part.astype(jnp.bfloat16), 'pcol')]
  transfers between devices with their start and end apart: 6 -> 5, of which waited for: 5 -> 4; matrix products, arithmetic and copies ran while one was open for 3% -> 3% of each run, Pallas kernels for 0% -> 0%
where the time goes in v1:
time: 429 us; the launch traced here: 428 us
  waiting for transfers between devices  274 us (64%)
  blocking collectives  119 us (28%)
  between operations  14.1 us (3%)
  matrix products  10.8 us (3%)
  local copies, waits for them, and re-layouts  7.12 us (2%)
    psum x1, waiting for transfers between devices, body(): diagonal_all = lax.psum(partial_diag, ('prow', 'pcol'))  130 us
    reduce_scatter x1, waiting for transfers between devices, body(): lax.psum_scatter(cross.astype(jnp.bfloat16), 'prow', scatter_dimension=0,...  60.5 us
    reduce_scatter x1, waiting for transfers between devices, body(): lax.psum_scatter(quadratic_two.astype(jnp.bfloat16), 'prow', scatter_dime...  57.2 us
    all_gather x1, blocking collectives, body(): spread_all = lax.all_gather(spread_one, 'prow', axis=0, tiled=True)  31.9 us
    all_gather x1, blocking collectives, body(): lax.all_gather(spread_two, 'prow', axis=0, tiled=True)  31.5 us
    all_gather x1, blocking collectives, body(): lax.all_gather(scaled_parent, 'prow', axis=0, tiled=True)  26.4 us
    psum x1, waiting for transfers between devices, body(): lax.psum(partial_two.astype(jnp.bfloat16), 'pcol').astype(jnp.float32)  26.2 us
    psum x1, blocking collectives, body(): lax.psum(quadratic_part.astype(jnp.bfloat16), 'pcol').astype(jnp.float32)  10.8 us
  transfers between devices with their start and end apart: 5, of which 4 were waited for; matrix products, arithmetic and copies ran while one was open for 3% of the time, Pallas kernels for 0%

profile of v1, /device:TPU:0, one launch (start us, length us, event | category | flops | bytes accessed | tf_op | source)
XLA Modules:
  0.0 428.4 jit_solution(16851071466511964490)
XLA Ops:
  7.2 1.1 fusion.10
  8.4 7.2 %all-gather = bf16[8,128,128]{2,1,0:T(8,128)(2,1)S(1)} all-gather(bf16[2,128,128]{2,1,0:T(8,128)(2,1)S(1)} %copy.72), channel_id=2, replica_groups=mesh['prow'=8,'pcol'=4] {'pcol'}, dimensions={0}, use_global_device_ids=true | all-gather | bytes 327680 | tf_op jit(solution)/shard_map/all_gather | solution.py:44
  16.0 31.9 %all-gather.1 = bf16[16,128,128]{2,1,0:T(8,128)(2,1)S(1)} all-gather(bf16[2,128,128]{2,1,0:T(8,128)(2,1)S(1)} %copy.74), channel_id=3, replica_groups=mesh['prow'=8,'pcol'=4] {'prow'}, dimensions={0}, use_global_device_ids=true | all-gather | bytes 589824 | tf_op jit(solution)/shard_map/all_gather | solution.py:50
  47.9 1.1 fusion.7
  50.5 5.8 %all-gather.2 = bf16[8,128,128]{2,1,0:T(8,128)(2,1)S(1)} all-gather(bf16[2,128,128]{2,1,0:T(8,128)(2,1)S(1)} %copy.79), channel_id=4, replica_groups=mesh['prow'=8,'pcol'=4] {'pcol'}, dimensions={0}, use_global_device_ids=true | all-gather | bytes 327680 | tf_op jit(solution)/shard_map/all_gather | solution.py:81
  56.6 31.5 %all-gather.3 = bf16[16,128,128]{2,1,0:T(8,128)(2,1)S(1)} all-gather(bf16[2,128,128]{2,1,0:T(8,128)(2,1)S(1)} %copy.81), channel_id=5, replica_groups=mesh['prow'=8,'pcol'=4] {'prow'}, dimensions={0}, use_global_device_ids=true | all-gather | bytes 589824 | tf_op jit(solution)/shard_map/all_gather | solution.py:98
  88.3 26.4 %all-gather.4 = bf16[1024,128]{0,1:T(8,128)(2,1)S(1)} all-gather(bf16[128,128]{0,1:T(8,128)(2,1)S(1)} %bitcast.158), channel_id=6, replica_groups=mesh['prow'=8,'pcol'=4] {'prow'}, dimensions={0}, use_global_device_ids=true | all-gather | bytes 294912 | tf_op jit(solution)/shard_map/all_gather | solution.py:99
  115.4 1.1 fusion.110
  117.2 0.9 fusion.9
  118.2 0.9 copy-done.1
  121.3 0.9 copy.92
  122.2 1.0 fusion.6
  123.3 26.2 %all-reduce.8.cloned.1.call-done = bf16[1,8,128,128]{2,3,1,0:T(8,128)(2,1)} async-done(((bf16[1,8,128,128]{2,3,1,0:T(8,128)(2,1)}), bf16[1,8,128,128]{2,3,1,0:T(8,128)(2,1)}) %all-reduce.8.cloned.1.call-update) | async-done | bytes 262160 | tf_op jit(solution)/shard_map/psum | solution.py:114
  149.5 1.1 fusion.21
  150.6 0.9 copy.93
  151.8 1.0 fusion.3
  152.8 129.8 %all-reduce.6.cloned.1.call-done = f32[8,128,128]{2,1,0:T(8,128)} async-done(((f32[8,128,128]{2,1,0:T(8,128)}), f32[8,128,128]{2,1,0:T(8,128)}) %all-reduce.6.cloned.1.call-update) | async-done | bytes 524304 | tf_op jit(solution)/shard_map/psum | solution.py:71
  282.6 1.8 fusion.23
  284.5 1.5 constant_dynamic-slice_fusion.3
  285.9 60.5 %reduce-scatter.3.cloned.1.call-done = bf16[1,128,128]{2,1,0:T(8,128)(2,1)} async-done(((bf16[8,128,128]{2,1,0:T(8,128)(2,1)}), bf16[1,128,128]{2,1,0:T(8,128)(2,1)}) %reduce-scatter.3.cloned.1.call-update) | async-done | bytes 32784 | tf_op jit(solution)/shard_map/reduce_scatter | solution.py:127
  346.4 5.6 %all-gather.5 = bf16[4,128,128]{2,1,0:T(8,128)(2,1)S(1)} all-gather(bf16[1,128,128]{2,1,0:T(8,128)(2,1)} %reduce-scatter.3.cloned.1.call-done), channel_id=7, replica_groups=mesh['prow'=8,'pcol'=4] {'pcol'}, dimensions={0}, use_global_device_ids=true | all-gather | bytes 163840 | tf_op jit(solution)/shard_map/all_gather | solution.py:135
  353.1 57.2 %reduce-scatter.5.cloned.1.call-done = bf16[1,128,128]{2,1,0:T(8,128)(2,1)} async-done(((bf16[8,128,128]{2,1,0:T(8,128)(2,1)}), bf16[1,128,128]{2,1,0:T(8,128)(2,1)}) %reduce-scatter.5.cloned.1.call-update) | async-done | bytes 32784 | tf_op jit(solution)/shard_map/reduce_scatter | solution.py:130
  410.3 10.8 %psum.31 = bf16[1,128,128]{2,1,0:T(8,128)(2,1)S(1)} all-reduce(bf16[1,128,128]{2,1,0:T(8,128)(2,1)} %reduce-scatter.5.cloned.1.call-done), channel_id=1, replica_groups=mesh['prow'=8,'pcol'=4] {'pcol'}, use_global_device_ids=true, to_apply=%region_9.10 | all-reduce | flops 16384 | bytes 65536 | tf_op jit(solution)/shard_map/psum | solution.py:138
  421.1 0.8 fusion.14
  (63 shorter events, 7.6 us)
Async XLA Ops:
  7.2 40.7 %copy-start = (bf16[1,2,128,128]{3,2,1,0:T(8,128)(2,1)S(1)}, bf16[1,2,128,128]{3,2,1,0:T(8,128)(2,1)}, u32[]{:S(2)}) copy-start(bf16[1,2,128,128]{3,2,1,0:T(8,128)(2,1)} %param.9) | copy-start | bytes 196612
  7.2 108.2 %all-reduce.4.cloned.1.call-start = ((), (), s32[]{:S(2)}) async-start(), calls=%async_computation.2 | async-start | bytes 524288 | tf_op jit(solution)/shard_map/psum | solution.py:54
  8.4 7.2 %copy-start.8 = (s32[8,8]{1,0:T(8,128)S(1)}, s32[8,8]{1,0:T(8,128)}, u32[]{:S(2)}) copy-start(s32[8,8]{1,0:T(8,128)} %param.12) | copy-start | bytes 772
  48.9 100.5 %all-reduce.8.cloned.1.call-start = ((), (), s32[]{:S(2)}) async-start(), calls=%async_computation.4 | async-start | bytes 524288 | tf_op jit(solution)/shard_map/psum | solution.py:114
  49.1 0.7 copy-start.10
  49.1 0.8 copy-start.9
  49.1 1.0 copy-start.6
  49.4 0.8 copy-start.4
  56.6 31.5 %copy-start.7 = (bf16[1,128,128]{2,1,0:T(8,128)(2,1)S(1)}, bf16[1,128,128]{2,1,0:T(8,128)(2,1)}, u32[]{:S(2)}) copy-start(bf16[1,128,128]{2,1,0:T(8,128)(2,1)} %param.14) | copy-start | bytes 98308
  118.1 0.9 copy-start.1
  118.1 164.5 %all-reduce.6.cloned.1.call-start = ((), (), s32[]{:S(2)}) async-start(), calls=%async_computation.3 | async-start | bytes 1048576 | tf_op jit(solution)/shard_map/psum | solution.py:71
  119.4 0.8 copy-start.5
  120.3 0.8 copy-start.2
  121.1 225.3 %reduce-scatter.3.cloned.1.call-start = ((), (), s32[]{:S(2)}) async-start(), calls=%async_computation.5 | async-start | bytes 294912 | tf_op jit(solution)/shard_map/reduce_scatter | solution.py:127
  123.2 287.1 %reduce-scatter.5.cloned.1.call-start = ((), (), s32[]{:S(2)}) async-start(), calls=%async_computation.6 | async-start | bytes 294912 | tf_op jit(solution)/shard_map/reduce_scatter | solution.py:130
  150.5 1.0 copy-start.3
Sparse Core Ops, SparseCore 0:
  49.1 32.7 all-reduce.3
  118.3 31.1 all-reduce.7
  154.8 127.7 all-reduce.5
  286.1 60.2 reduce-scatter.2
  350.0 60.2 reduce-scatter.4
